TPU v7x, 128 devices: a whole 4x4x4 slice. The times are simulated.
128 devices in a mesh: row: 8 (over y_hi, x), col: 16 (over y_lo, z, core).
Axes of the slice: x: 4, y: 4 (y_hi: 2, y_lo: 2; y = y_hi * 2 + y_lo), z: 4, core: 2. Of those that a mesh axis runs over, the one named last changes fastest.
Arguments:
- right_side: float32 [16, 512, 512], P('col', 'row'), may hold values from -6 to 6
- affinity_blocks: float32 [16, 16, 8, 128, 128], P('row', 'col'), may hold values from -0.03125 to 0.03125
- block_coords: int32 [16, 16, 8, 2], P('row', 'col'), may hold values from 0 to 3
- block_counts: int32 [16, 16], P('row', 'col'), may hold values from 4 to 8, as said below
Outputs:
- ranking: float32 [16, 512, 512], P('col', 'row')
- residual: float32 [16, 512, 512], P('col', 'row')
Inputs may be any that keep to these rules, and one draw needn't show every extreme that they name: `block_counts`: some grid tile holds 8 live blocks in every draw.
All inputs are finite; a program needn't handle non-finite values.
Results may differ from a plain program's by a relative error of at most 0.0003.
Values sent between devices are 32-bit elements; how exact they have to be, the bound alone decides.
No kernel may reach another device: no remote copies, remote signals or barrier semaphores. Data moves between devices by JAX's collectives and lax.ppermute only.
A program may use at most 64 MiB of HBM per device.

v0:
```python
import jax
import jax.numpy as jnp
from jax import lax
from jax.sharding import PartitionSpec as P

ITERS = 3
diffusion = 0.8


def broadcast(value, axis, source):
    kept = jnp.where(lax.axis_index(axis) == source, value, 0).astype(value.dtype)
    return lax.psum(kept, axis)


def live_blocks(blocks, count):
    live = (jnp.arange(blocks.shape[0], dtype=jnp.int32) < count).astype(blocks.dtype)
    return blocks * live[:, None, None]


def forward_only(masked, rows, cols, column_field):
    position = jnp.arange(column_field.shape[0], dtype=jnp.int32)
    picked = jnp.take(column_field, cols, axis=0)
    product = jnp.einsum("kab,kbw->kaw", masked, picked, precision=lax.Precision.HIGHEST)
    row_onehot = (rows[None, :] == position[:, None]).astype(jnp.float32)
    return jnp.einsum("tk,kaw->taw", row_onehot, product, precision=lax.Precision.HIGHEST)


def backward_only(masked, rows, cols, row_field):
    position = jnp.arange(row_field.shape[0], dtype=jnp.int32)
    chosen = jnp.take(row_field, rows, axis=0)
    mirrored = jnp.einsum("kab,kaw->kbw", masked, chosen, precision=lax.Precision.HIGHEST)
    col_onehot = (cols[None, :] == position[:, None]).astype(jnp.float32)
    return jnp.einsum("tk,kbw->tbw", col_onehot, mirrored, precision=lax.Precision.HIGHEST)


def tile_products(masked, rows, cols, column_field, row_field):
    forward = forward_only(masked, rows, cols, column_field)
    backward = backward_only(masked, rows, cols, row_field)
    return (forward, backward)


def block_products(affinity_blocks, block_coords, block_counts, column_block, row_blocks):
    members = affinity_blocks.shape[0]
    edge = affinity_blocks.shape[-1]
    width = column_block.shape[1]
    column_field = column_block.reshape(-1, edge, width)
    forward_parts = []
    backward_total = jnp.zeros(column_field.shape, jnp.float32)
    for member in range(members):
        masked = live_blocks(affinity_blocks[member, 0], block_counts[member, 0])
        forward, backward = tile_products(
            masked,
            block_coords[member, 0, :, 0],
            block_coords[member, 0, :, 1],
            column_field,
            row_blocks[member].reshape(column_field.shape),
        )
        forward_parts.append(forward.reshape(column_block.shape))
        backward_total = backward_total + backward
    return (jnp.stack(forward_parts), backward_total.reshape(column_block.shape))


def operate(piece, affinity_blocks, block_coords, block_counts):
    rows_count = lax.axis_size("row")
    cols_count = lax.axis_size("col")
    members = cols_count // rows_count
    my_row = lax.axis_index("row")
    share = piece.shape[1]
    width = piece.shape[2]
    sliver = share // cols_count
    whole = lax.all_gather(piece, "row", axis=1, tiled=True)
    received = []
    for member in range(members):
        received.append(broadcast(whole[0], "col", my_row * members + member))
    row_blocks = jnp.stack(received)
    forward, backward = block_products(
        affinity_blocks, block_coords, block_counts, whole[0], row_blocks
    )
    back_part = lax.psum_scatter(backward[None], "row", scatter_dimension=1, tiled=True)
    spread = forward.reshape(members, rows_count, cols_count, sliver, width)
    summed = lax.psum_scatter(spread, "col", scatter_dimension=2, tiled=True)
    ordered = summed.reshape(members, rows_count, sliver, width).transpose(1, 0, 2, 3)
    ordered = ordered.reshape(rows_count * members, sliver, width)
    forward_part = lax.all_to_all(
        lax.all_to_all(ordered, "row", split_axis=0, concat_axis=0, tiled=True),
        "col",
        split_axis=0,
        concat_axis=1,
        tiled=True,
    )
    return piece - diffusion * (forward_part + back_part)


def squares(residual):
    return lax.psum(jnp.sum(residual * residual, axis=(0, 1)), ("row", "col"))


def shards(right_side, affinity_blocks, block_coords, block_counts):
    ranking = jnp.zeros_like(right_side)
    residual = right_side
    direction = right_side
    norm_now = squares(residual)
    for step in range(ITERS):
        image = operate(direction, affinity_blocks, block_coords, block_counts)
        curve = lax.psum(jnp.sum(direction * image, axis=(0, 1)), ("row", "col"))
        alpha = norm_now / curve
        ranking = ranking + alpha * direction
        residual = residual - alpha * image
        if step + 1 < ITERS:
            norm_next = squares(residual)
            direction = residual + norm_next / norm_now * direction
            norm_now = norm_next
    return (ranking, residual)


def solution(mesh):
    in_specs = (
        P("col", "row", None),
        P("row", "col", None, None, None),
        P("row", "col", None, None),
        P("row", "col"),
    )
    out_specs = (P("col", "row", None), P("col", "row", None))
    return jax.shard_map(shards, mesh=mesh, in_specs=in_specs, out_specs=out_specs, check_vma=False)
```

profile of v0, /device:TPU:1, one launch (start us, length us, event | category | flops | bytes accessed | tf_op | source)
XLA Modules:
  0.0 1282.6 jit_solution(11291299337467463532)
XLA Ops:
  9.9 50.0 %all-gather.4.cloned.1.call-done = f32[1,512,512]{2,1,0:T(8,128)} async-done(((f32[1,64,512]{2,1,0:T(8,128)}), f32[1,512,512]{2,1,0:T(8,128)}) %all-gather.4.cloned.1.call-update) | async-done | bytes 1048592 | tf_op jit(solution)/shard_map/all_gather | solution.py:71
  60.0 2.9 broadcast_select_fusion.5
  63.8 2.1 gather_fusion.1
  65.9 3.6 fusion.44
  69.5 2.2 fusion.20
  75.3 3.6 fusion.46
  79.0 2.2 fusion.22
  84.6 2.6 copy.49
  87.5 98.5 %all-reduce.12.cloned.1.call-done = (f32[4,128,512]{2,1,0:T(8,128)}, f32[4,128,512]{2,1,0:T(8,128)}) async-done(((f32[4,128,512]{2,1,0:T(8,128)}, f32[4,128,512]{2,1,0:T(8,128)}), (f32[4,128,512]{2,1,0:T(8,128)}, f32[4,128,512]{2,1,0:T(8,128)})) %all-reduce.12.cloned.1.call-update) | async-done | bytes 2097168 | tf_op jit(solution)/shard_map/psum | solution.py:12
  186.0 3.2 gather_fusion.3
  191.2 3.7 fusion.40
  194.9 2.2 fusion.16
  197.1 2.2 fusion.42
  199.3 2.3 fusion.48
  203.0 46.3 %reduce-scatter.7.cloned.1.call-done = f32[2,8,1,4,512]{4,1,3,0,2:T(8,128)} async-done(((f32[2,8,16,4,512]{4,1,3,0,2:T(8,128)}), f32[2,8,1,4,512]{4,1,3,0,2:T(8,128)}) %reduce-scatter.7.cloned.1.call-update) | async-done | bytes 131088 | tf_op jit(solution)/shard_map/reduce_scatter | solution.py:81
  250.3 13.3 %all_to_all.51 = f32[16,4,512]{2,1,0:T(4,128)S(1)} all-to-all(f32[16,4,512]{2,1,0:T(4,128)S(1)} %bitcast.97), channel_id=1, replica_groups=mesh['row'=8,'col'=16] {'row'}, dimensions={0} | all-to-all | bytes 262144 | tf_op jit(solution)/shard_map/all_to_all | solution.py:85
  263.6 14.2 %all_to_all.52 = f32[16,4,512]{2,1,0:T(4,128)S(1)} all-to-all(f32[16,4,512]{2,1,0:T(4,128)S(1)} %all_to_all.51), channel_id=1, replica_groups=mesh['row'=8,'col'=16] {'col'}, dimensions={0} | all-to-all | bytes 262144 | tf_op jit(solution)/shard_map/all_to_all | solution.py:84
  277.8 47.4 %reduce-scatter.9.cloned.1.call-done = f32[1,64,512]{2,1,0:T(8,128)} async-done(((f32[1,512,512]{2,1,0:T(8,128)}), f32[1,64,512]{2,1,0:T(8,128)}) %reduce-scatter.9.cloned.1.call-update) | async-done | bytes 131088 | tf_op jit(solution)/shard_map/reduce_scatter | solution.py:79
  326.1 66.3 %all-reduce = (f32[512]{0:T(512)S(1)}, f32[512]{0:T(512)S(1)}) all-reduce(f32[512]{0:T(512)S(1)} %get-tuple-element.4, f32[512]{0:T(512)S(1)} %get-tuple-element.3), channel_id=1, replica_groups=mesh['row'=8,'col'=16] {'row','col'}, use_global_device_ids=true, to_apply=%region_1.0 | all-reduce | flops 1024 | bytes 8192 | tf_op jit(solution)/shard_map/psum | solution.py:95
  393.4 62.5 %psum.88 = f32[512]{0:T(512)S(1)} all-reduce(f32[512]{0:T(512)S(1)} %get-tuple-element.15), channel_id=1, replica_groups=mesh['row'=8,'col'=16] {'row','col'}, use_global_device_ids=true, to_apply=%region_9.11 | all-reduce | flops 512 | bytes 4096 | tf_op jit(solution)/shard_map/psum | solution.py:95
  456.7 43.6 %all-gather.6.cloned.1.call-done = f32[1,512,512]{2,1,0:T(8,128)} async-done(((f32[1,64,512]{2,1,0:T(8,128)}), f32[1,512,512]{2,1,0:T(8,128)}) %all-gather.6.cloned.1.call-update) | async-done | bytes 1048592 | tf_op jit(solution)/shard_map/all_gather | solution.py:71
  500.3 2.9 broadcast_select_fusion.3
  503.8 2.1 gather_fusion.5
  505.8 2.1 gather_fusion.4
  507.9 3.6 fusion.36
  511.5 2.2 fusion.12
  515.1 2.5 stack.25
  517.6 2.0 fusion.38
  519.7 2.2 fusion.14
  525.3 2.6 copy.60
  528.2 98.3 %all-reduce.10.cloned.1.call-done = (f32[4,128,512]{2,1,0:T(8,128)}, f32[4,128,512]{2,1,0:T(8,128)}) async-done(((f32[4,128,512]{2,1,0:T(8,128)}, f32[4,128,512]{2,1,0:T(8,128)}), (f32[4,128,512]{2,1,0:T(8,128)}, f32[4,128,512]{2,1,0:T(8,128)})) %all-reduce.10.cloned.1.call-update) | async-done | bytes 2097168 | tf_op jit(solution)/shard_map/psum | solution.py:12
  626.4 3.2 gather_fusion.7
  631.6 3.7 fusion.32
  635.3 2.2 fusion.8
  637.5 2.2 fusion.34
  639.7 2.3 fusion.51
  643.4 46.4 %reduce-scatter.11.cloned.1.call-done = f32[2,8,1,4,512]{4,1,3,0,2:T(8,128)} async-done(((f32[2,8,16,4,512]{4,1,3,0,2:T(8,128)}), f32[2,8,1,4,512]{4,1,3,0,2:T(8,128)}) %reduce-scatter.11.cloned.1.call-update) | async-done | bytes 131088 | tf_op jit(solution)/shard_map/reduce_scatter | solution.py:81
  690.8 13.3 %all_to_all.53 = f32[16,4,512]{2,1,0:T(4,128)S(1)} all-to-all(f32[16,4,512]{2,1,0:T(4,128)S(1)} %bitcast.98), channel_id=1, replica_groups=mesh['row'=8,'col'=16] {'row'}, dimensions={0} | all-to-all | bytes 262144 | tf_op jit(solution)/shard_map/all_to_all | solution.py:85
  704.1 14.3 %all_to_all.54 = f32[16,4,512]{2,1,0:T(4,128)S(1)} all-to-all(f32[16,4,512]{2,1,0:T(4,128)S(1)} %all_to_all.53), channel_id=1, replica_groups=mesh['row'=8,'col'=16] {'col'}, dimensions={0} | all-to-all | bytes 262144 | tf_op jit(solution)/shard_map/all_to_all | solution.py:84
  718.4 47.8 %reduce-scatter.13.cloned.1.call-done = f32[1,64,512]{2,1,0:T(8,128)} async-done(((f32[1,512,512]{2,1,0:T(8,128)}), f32[1,64,512]{2,1,0:T(8,128)}) %reduce-scatter.13.cloned.1.call-update) | async-done | bytes 131088 | tf_op jit(solution)/shard_map/reduce_scatter | solution.py:79
  767.2 66.3 %psum.91 = f32[512]{0:T(512)S(1)} all-reduce(f32[512]{0:T(512)S(1)} %multiply_reduce_fusion.2), channel_id=1, replica_groups=mesh['row'=8,'col'=16] {'row','col'}, use_global_device_ids=true, to_apply=%region_15.17 | all-reduce | flops 512 | bytes 4096 | tf_op jit(solution)/shard_map/psum | solution.py:105
  834.5 62.5 %psum.92 = f32[512]{0:T(512)S(1)} all-reduce(f32[512]{0:T(512)S(1)} %get-tuple-element.13), channel_id=1, replica_groups=mesh['row'=8,'col'=16] {'row','col'}, use_global_device_ids=true, to_apply=%region_17.19 | all-reduce | flops 512 | bytes 4096 | tf_op jit(solution)/shard_map/psum | solution.py:95
  897.8 43.6 %all-gather.8.cloned.1.call-done = f32[1,512,512]{2,1,0:T(8,128)} async-done(((f32[1,64,512]{2,1,0:T(8,128)}), f32[1,512,512]{2,1,0:T(8,128)}) %all-gather.8.cloned.1.call-update) | async-done | bytes 1048592 | tf_op jit(solution)/shard_map/all_gather | solution.py:71
  941.4 3.0 broadcast_select_fusion.1
  944.8 2.2 gather_fusion.9
  947.0 2.3 gather_fusion.8
  949.4 3.6 fusion.28
  953.0 2.2 fusion.4
  956.6 2.5 stack.28
  959.1 2.0 fusion.30
  961.1 2.2 fusion.6
  966.8 2.6 copy.71
  969.6 97.9 %all-reduce.8.cloned.1.call-done = (f32[4,128,512]{2,1,0:T(8,128)}, f32[4,128,512]{2,1,0:T(8,128)}) async-done(((f32[4,128,512]{2,1,0:T(8,128)}, f32[4,128,512]{2,1,0:T(8,128)}), (f32[4,128,512]{2,1,0:T(8,128)}, f32[4,128,512]{2,1,0:T(8,128)})) %all-reduce.8.cloned.1.call-update) | async-done | bytes 2097168 | tf_op jit(solution)/shard_map/psum | solution.py:12
  1067.5 3.4 gather_fusion.11
  1070.8 2.0 gather_fusion.10
  1072.9 3.7 fusion.24
  1076.6 2.2 fusion
  1078.9 2.2 fusion.26
  1081.0 2.3 fusion.54
  1084.7 46.0 %reduce-scatter.15.cloned.1.call-done = f32[2,8,1,4,512]{4,1,3,0,2:T(8,128)} async-done(((f32[2,8,16,4,512]{4,1,3,0,2:T(8,128)}), f32[2,8,1,4,512]{4,1,3,0,2:T(8,128)}) %reduce-scatter.15.cloned.1.call-update) | async-done | bytes 131088 | tf_op jit(solution)/shard_map/reduce_scatter | solution.py:81
  1131.8 13.3 %all_to_all.55 = f32[16,4,512]{2,1,0:T(4,128)S(1)} all-to-all(f32[16,4,512]{2,1,0:T(4,128)S(1)} %bitcast.99), channel_id=1, replica_groups=mesh['row'=8,'col'=16] {'row'}, dimensions={0} | all-to-all | bytes 262144 | tf_op jit(solution)/shard_map/all_to_all | solution.py:85
  1145.0 14.2 %all_to_all.56 = f32[16,4,512]{2,1,0:T(4,128)S(1)} all-to-all(f32[16,4,512]{2,1,0:T(4,128)S(1)} %all_to_all.55), channel_id=1, replica_groups=mesh['row'=8,'col'=16] {'col'}, dimensions={0} | all-to-all | bytes 262144 | tf_op jit(solution)/shard_map/all_to_all | solution.py:84
  1159.3 47.4 %reduce-scatter.17.cloned.1.call-done = f32[1,64,512]{2,1,0:T(8,128)} async-done(((f32[1,512,512]{2,1,0:T(8,128)}), f32[1,64,512]{2,1,0:T(8,128)}) %reduce-scatter.17.cloned.1.call-update) | async-done | bytes 131088 | tf_op jit(solution)/shard_map/reduce_scatter | solution.py:79
  1207.6 66.3 %psum.95 = f32[512]{0:T(512)S(1)} all-reduce(f32[512]{0:T(512)S(1)} %multiply_reduce_fusion), channel_id=1, replica_groups=mesh['row'=8,'col'=16] {'row','col'}, use_global_device_ids=true, to_apply=%region_23.25 | all-reduce | flops 512 | bytes 4096 | tf_op jit(solution)/shard_map/psum | solution.py:105
  (143 shorter events, 40.8 us)
Async XLA Ops:
  7.2 52.8 %all-gather.4.cloned.1.call-start = ((), (), s32[]{:S(2)}) async-start(), calls=%async_computation.12 | async-start | bytes 1179648 | tf_op jit(solution)/shard_map/all_gather | solution.py:71
  7.9 178.1 %all-reduce.12.cloned.1.call-start = ((), (), s32[]{:S(2)}) async-start(), calls=%async_computation.23 | async-start | bytes 4194304 | tf_op jit(solution)/shard_map/psum | solution.py:12
  9.9 53.7 %copy-start.26 = (s32[2,1,8,2]{2,3,1,0:T(2,128)S(1)}, s32[2,1,8,2]{2,3,1,0:T(2,128)}, u32[]{:S(2)}) copy-start(s32[2,1,8,2]{2,3,1,0:T(2,128)} %param.8) | copy-start | bytes 388
  60.0 3.8 copy-start.1
  62.9 186.4 %reduce-scatter.7.cloned.1.call-start = ((), (), s32[]{:S(2)}) async-start(), calls=%async_computation.13 | async-start | bytes 2228224 | tf_op jit(solution)/shard_map/reduce_scatter | solution.py:81
  63.7 444.2 %copy-start.22 = (pred[8]{0:T(512)(128)(4,1)}, pred[8]{0:T(512)(128)(4,1)S(1)}, u32[]{:S(2)}) copy-start(pred[8]{0:T(512)(128)(4,1)S(1)} %get-tuple-element.37) | copy-start | bytes 28
  63.7 454.0 %copy-start.20 = (pred[8]{0:T(512)(128)(4,1)}, pred[8]{0:T(512)(128)(4,1)S(1)}, u32[]{:S(2)}) copy-start(pred[8]{0:T(512)(128)(4,1)S(1)} %get-tuple-element.41) | copy-start | bytes 28
  63.7 567.9 %copy-start.18 = (pred[8]{0:T(512)(128)(4,1)}, pred[8]{0:T(512)(128)(4,1)S(1)}, u32[]{:S(2)}) copy-start(pred[8]{0:T(512)(128)(4,1)S(1)} %get-tuple-element.39) | copy-start | bytes 28
  63.7 573.8 %copy-start.16 = (pred[8]{0:T(512)(128)(4,1)}, pred[8]{0:T(512)(128)(4,1)S(1)}, u32[]{:S(2)}) copy-start(pred[8]{0:T(512)(128)(4,1)S(1)} %get-tuple-element.17) | copy-start | bytes 28
  63.7 440.0 %copy-start.36 = (s32[1024]{0:T(1024)}, s32[1024]{0:T(1024)S(1)}, u32[]{:S(2)}) copy-start(s32[1024]{0:T(1024)S(1)} %get-tuple-element.47) | copy-start | bytes 12292
  63.7 442.1 %copy-start.35 = (s32[1024]{0:T(1024)}, s32[1024]{0:T(1024)S(1)}, u32[]{:S(2)}) copy-start(s32[1024]{0:T(1024)S(1)} %get-tuple-element.48) | copy-start | bytes 12292
  63.8 447.8 %copy-start.31 = (s32[8]{0:T(128)}, s32[8]{0:T(128)S(1)}, u32[]{:S(2)}) copy-start(s32[8]{0:T(128)S(1)} %get-tuple-element.36) | copy-start | bytes 100
  63.8 455.9 %copy-start.29 = (s32[8]{0:T(128)}, s32[8]{0:T(128)S(1)}, u32[]{:S(2)}) copy-start(s32[8]{0:T(128)S(1)} %get-tuple-element.34) | copy-start | bytes 100
  63.8 571.5 %copy-start.27 = (s32[8]{0:T(128)}, s32[8]{0:T(128)S(1)}, u32[]{:S(2)}) copy-start(s32[8]{0:T(128)S(1)} %get-tuple-element.35) | copy-start | bytes 100
  63.8 575.9 %copy-start.24 = (s32[8]{0:T(128)}, s32[8]{0:T(128)S(1)}, u32[]{:S(2)}) copy-start(s32[8]{0:T(128)S(1)} %get-tuple-element.33) | copy-start | bytes 100
  63.8 2.1 copy-start
  81.2 1.7 copy-start.7
  87.2 238.0 %reduce-scatter.9.cloned.1.call-start = ((), (), s32[]{:S(2)}) async-start(), calls=%async_computation.14 | async-start | bytes 1179648 | tf_op jit(solution)/shard_map/reduce_scatter | solution.py:79
  87.5 539.0 %copy-start.34 = (s32[1024]{0:T(1024)}, s32[1024]{0:T(1024)S(1)}, u32[]{:S(2)}) copy-start(s32[1024]{0:T(1024)S(1)} %get-tuple-element.45) | copy-start | bytes 12292
  87.5 542.2 %copy-start.33 = (s32[1024]{0:T(1024)}, s32[1024]{0:T(1024)S(1)}, u32[]{:S(2)}) copy-start(s32[1024]{0:T(1024)S(1)} %get-tuple-element.46) | copy-start | bytes 12292
  201.6 123.6 %copy-start.10 = (f32[1,64,512]{2,1,0:T(8,128)S(1)}, f32[1,64,512]{2,1,0:T(8,128)}, u32[]{:S(2)}) copy-start(f32[1,64,512]{2,1,0:T(8,128)} %param.6) | copy-start | bytes 393220
  202.9 297.4 %all-gather.6.cloned.1.call-start = ((), (), s32[]{:S(2)}) async-start(), calls=%async_computation.15 | async-start | bytes 1179648 | tf_op jit(solution)/shard_map/all_gather | solution.py:71
  456.7 169.7 %all-reduce.10.cloned.1.call-start = ((), (), s32[]{:S(2)}) async-start(), calls=%async_computation.22 | async-start | bytes 4194304 | tf_op jit(solution)/shard_map/psum | solution.py:12
  500.3 3.4 copy-start.3
  503.3 186.5 %reduce-scatter.11.cloned.1.call-start = ((), (), s32[]{:S(2)}) async-start(), calls=%async_computation.16 | async-start | bytes 2228224 | tf_op jit(solution)/shard_map/reduce_scatter | solution.py:81
  513.7 3.9 copy-start.5
  521.9 1.7 copy-start.9
  527.9 238.3 %reduce-scatter.13.cloned.1.call-start = ((), (), s32[]{:S(2)}) async-start(), calls=%async_computation.17 | async-start | bytes 1179648 | tf_op jit(solution)/shard_map/reduce_scatter | solution.py:79
  642.0 124.2 %copy-start.6 = (f32[1,64,512]{2,1,0:T(8,128)S(1)}, f32[1,64,512]{2,1,0:T(8,128)}, u32[]{:S(2)}) copy-start(f32[1,64,512]{2,1,0:T(8,128)} %multiply_add_fusion.2) | copy-start | bytes 393220
  643.4 298.0 %all-gather.8.cloned.1.call-start = ((), (), s32[]{:S(2)}) async-start(), calls=%async_computation.18 | async-start | bytes 1179648 | tf_op jit(solution)/shard_map/all_gather | solution.py:71
  833.5 64.3 %copy-start.14 = (f32[512]{0:T(512)}, f32[512]{0:T(512)S(1)}, u32[]{:S(2)}) copy-start(f32[512]{0:T(512)S(1)} %div.17) | copy-start | bytes 6148
  834.5 63.3 %copy-start.12 = (f32[1,64,512]{2,1,0:T(8,128)}, f32[1,64,512]{2,1,0:T(8,128)S(1)}, u32[]{:S(2)}) copy-start(f32[1,64,512]{2,1,0:T(8,128)S(1)} %get-tuple-element.14) | copy-start | bytes 393220
  897.8 169.7 %all-reduce.8.cloned.1.call-start = ((), (), s32[]{:S(2)}) async-start(), calls=%async_computation.21 | async-start | bytes 4194304 | tf_op jit(solution)/shard_map/psum | solution.py:12
  941.4 3.4 copy-start.2
  944.4 186.4 %reduce-scatter.15.cloned.1.call-start = ((), (), s32[]{:S(2)}) async-start(), calls=%async_computation.19 | async-start | bytes 2228224 | tf_op jit(solution)/shard_map/reduce_scatter | solution.py:81
  947.0 2.3 copy-start.23
  949.4 3.6 copy-start.32
  955.2 3.9 copy-start.4
  955.2 3.9 copy-start.21
  959.1 2.0 copy-start.30
  963.3 1.7 copy-start.8
  969.4 237.3 %reduce-scatter.17.cloned.1.call-start = ((), (), s32[]{:S(2)}) async-start(), calls=%async_computation.20 | async-start | bytes 1179648 | tf_op jit(solution)/shard_map/reduce_scatter | solution.py:79
  1070.8 2.0 copy-start.19
  1072.9 3.7 copy-start.28
  1076.6 2.2 copy-start.17
  1078.9 2.2 copy-start.25
  1083.4 123.3 %copy-start.11 = (f32[1,64,512]{2,1,0:T(8,128)S(1)}, f32[1,64,512]{2,1,0:T(8,128)}, u32[]{:S(2)}) copy-start(f32[1,64,512]{2,1,0:T(8,128)} %multiply_add_fusion.1) | copy-start | bytes 393220
  1083.4 190.5 %copy-start.13 = (f32[1,64,512]{2,1,0:T(8,128)S(1)}, f32[1,64,512]{2,1,0:T(8,128)}, u32[]{:S(2)}) copy-start(f32[1,64,512]{2,1,0:T(8,128)} %copy-done.12) | copy-start | bytes 393220
  1083.4 190.5 %copy-start.15 = (f32[512]{0:T(512)S(1)}, f32[512]{0:T(512)}, u32[]{:S(2)}) copy-start(f32[512]{0:T(512)} %copy-done.14) | copy-start | bytes 6148
Sparse Core Ops, SparseCore 0:
  10.3 49.5 all-gather.3
  63.0 122.9 all-reduce.11
  188.4 60.8 reduce-scatter.6
  252.8 72.3 reduce-scatter.8
  456.8 43.4 all-gather.5
  503.4 122.9 all-reduce.9
  628.9 60.8 reduce-scatter.10
  693.9 72.3 reduce-scatter.12
  897.9 43.4 all-gather.7
  944.5 122.9 all-reduce.7
  1069.9 60.8 reduce-scatter.14
  1134.3 72.3 reduce-scatter.16
where the time goes:
time: 1290 us; the launch traced here: 1280 us
  waiting for transfers between devices  714 us (55%)
  blocking collectives  407 us (32%)
  matrix products  62.8 us (5%)
  local copies, waits for them, and re-layouts  59.1 us (5%)
  other arithmetic  23.3 us (2%)
  between operations  15.1 us (1%)
    psum x3, waiting for transfers between devices, broadcast(): return lax.psum(kept, axis)  295 us
    psum x3, blocking collectives, squares(): return lax.psum(jnp.sum(residual * residual, axis=(0, 1)), ('row', 'col'))  191 us
    reduce_scatter x3, waiting for transfers between devices, operate(): lax.psum_scatter(backward[None], 'row', scatter_dimension=1, tiled=True)  142 us
    reduce_scatter x3, waiting for transfers between devices, operate(): summed = lax.psum_scatter(spread, 'col', scatter_dimension=2, tiled=True)  139 us
    all_gather x3, waiting for transfers between devices, operate(): whole = lax.all_gather(piece, 'row', axis=1, tiled=True)  137 us
    psum x2, blocking collectives, shards(): curve = lax.psum(jnp.sum(direction * image, axis=(0, 1)), ('row', 'col'))  133 us
    all_to_all x3, blocking collectives, operate(): lax.all_to_all(lax.all_to_all(ordered, 'row', split_axis=0, concat_axis=0...  42.7 us
    all_to_all x3, blocking collectives, operate(): lax.all_to_all(ordered, 'row', split_axis=0, concat_axis=0, tiled=True)  39.9 us
  transfers between devices with their start and end apart: 12, of which 12 were waited for; matrix products, arithmetic and copies ran while one was open for 10% of the time, Pallas kernels for 0%

commit v1 on v0

--- a/solution.py
+++ b/solution.py
@@ -1,3 +1,4 @@
+import functools
 import jax
 import jax.numpy as jnp
 from jax import lax
@@ -5,6 +6,21 @@
 
 ITERS = 3
 diffusion = 0.8
+
+
+def advance_edges_now(frame, named_axis, at_axis, dim_no):
+    return jnp.concatenate(
+        lax.all_to_all(
+            jnp.stack(jnp.split(frame, lax.axis_size(named_axis), axis=at_axis), axis=0),
+            named_axis,
+            concat_axis=0,
+            split_axis=0,
+        ),
+        axis=dim_no,
+    )
+
+
+produce_seats_all = functools.partial(advance_edges_now, named_axis="col", at_axis=0, dim_no=1)
 
 
 def broadcast(value, axis, source):
@@ -81,12 +97,8 @@
     summed = lax.psum_scatter(spread, "col", scatter_dimension=2, tiled=True)
     ordered = summed.reshape(members, rows_count, sliver, width).transpose(1, 0, 2, 3)
     ordered = ordered.reshape(rows_count * members, sliver, width)
-    forward_part = lax.all_to_all(
-        lax.all_to_all(ordered, "row", split_axis=0, concat_axis=0, tiled=True),
-        "col",
-        split_axis=0,
-        concat_axis=1,
-        tiled=True,
+    forward_part = produce_seats_all(
+        lax.all_to_all(ordered, "row", split_axis=0, concat_axis=0, tiled=True)
     )
     return piece - diffusion * (forward_part + back_part)
 

time: 1290 us -> 1330 us (1.031)
  blocking collectives: 407 us -> 367 us
  waiting for transfers between devices: 714 us -> 749 us
  starting transfers between devices: 1.83 us -> 20.5 us
  local copies, waits for them, and re-layouts: 59.1 us -> 74.1 us
    all_to_all x6 -> x3, blocking collectives: 82.6 us -> 43 us  [advance_edges_now(): lax.all_to_all(jnp.stack(jnp.split(frame, lax.axis_size(named_axis), axis...]
    all_to_all x0 -> x3, starting transfers between devices: none -> 19.6 us  [operate(): lax.all_to_all(ordered, 'row', split_axis=0, concat_axis=0, tiled=True)]
    reduce_scatter x3, waiting for transfers between devices: 142 us -> 159 us  [operate(): lax.psum_scatter(backward[None], 'row', scatter_dimension=1, tiled=True)]
  transfers between devices with their start and end apart: 12 -> 15, of which waited for: 12 -> 15; matrix products, arithmetic and copies ran while one was open for 10% -> 11% of each run, Pallas kernels for 0% -> 0%
where the time goes in v1:
time: 1330 us; the launch traced here: 1310 us
  waiting for transfers between devices  749 us (56%)
  blocking collectives  367 us (28%)
  local copies, waits for them, and re-layouts  74.1 us (6%)
  matrix products  64.6 us (5%)
  other arithmetic  23.4 us (2%)
  starting transfers between devices  20.5 us (2%)
  between operations  15.5 us (1%)
    psum x3, waiting for transfers between devices, broadcast(): return lax.psum(kept, axis)  295 us
    psum x3, blocking collectives, squares(): return lax.psum(jnp.sum(residual * residual, axis=(0, 1)), ('row', 'col'))  191 us
    reduce_scatter x3, waiting for transfers between devices, operate(): lax.psum_scatter(backward[None], 'row', scatter_dimension=1, tiled=True)  159 us
    reduce_scatter x3, waiting for transfers between devices, operate(): summed = lax.psum_scatter(spread, 'col', scatter_dimension=2, tiled=True)  150 us
    all_gather x3, waiting for transfers between devices, operate(): whole = lax.all_gather(piece, 'row', axis=1, tiled=True)  137 us
    psum x2, blocking collectives, shards(): curve = lax.psum(jnp.sum(direction * image, axis=(0, 1)), ('row', 'col'))  133 us
    all_to_all x3, blocking collectives, advance_edges_now(): lax.all_to_all(jnp.stack(jnp.split(frame, lax.axis_size(named_axis), axis...  43 us
  transfers between devices with their start and end apart: 15, of which 15 were waited for; matrix products, arithmetic and copies ran while one was open for 11% of the time, Pallas kernels for 0%

profile of v1, /device:TPU:1, one launch (start us, length us, event | category | flops | bytes accessed | tf_op | source)
XLA Modules:
  0.0 1313.8 jit_solution(4854405425362829065)
XLA Ops:
  9.9 50.0 %all-gather.4.cloned.1.call-done = f32[1,512,512]{2,1,0:T(8,128)} async-done(((f32[1,64,512]{2,1,0:T(8,128)}), f32[1,512,512]{2,1,0:T(8,128)}) %all-gather.4.cloned.1.call-update) | async-done | bytes 1048592 | tf_op jit(solution)/shard_map/all_gather | solution.py:87
  60.0 3.0 broadcast_select_fusion.5
  65.9 3.6 fusion.44
  69.5 2.2 fusion.20
  75.4 3.6 fusion.46
  79.1 2.2 fusion.22
  84.7 2.6 copy.139
  87.3 98.7 %all-reduce.12.cloned.1.call-done = (f32[4,128,512]{2,1,0:T(8,128)}, f32[4,128,512]{2,1,0:T(8,128)}) async-done(((f32[4,128,512]{2,1,0:T(8,128)}, f32[4,128,512]{2,1,0:T(8,128)}), (f32[4,128,512]{2,1,0:T(8,128)}, f32[4,128,512]{2,1,0:T(8,128)})) %all-reduce.12.cloned.1.call-update) | async-done | bytes 2097168 | tf_op jit(solution)/shard_map/psum | solution.py:28
  186.1 2.2 gather_fusion.3
  188.3 3.2 gather_fusion.2
  191.6 2.1 fusion.40
  193.7 3.2 fusion.16
  197.0 2.1 fusion.42
  199.1 50.2 %reduce-scatter.7.cloned.1.call-done = f32[2,8,1,4,512]{4,1,3,0,2:T(8,128)} async-done(((f32[2,8,16,4,512]{4,1,3,0,2:T(8,128)}), f32[2,8,1,4,512]{4,1,3,0,2:T(8,128)}) %reduce-scatter.7.cloned.1.call-update) | async-done | bytes 131088 | tf_op jit(solution)/shard_map/reduce_scatter | solution.py:97
  251.0 6.5 all-to-all-start
  257.5 3.5 fusion.48
  264.6 14.3 %all_to_all.30 = f32[16,1,4,512]{3,2,1,0:T(4,128)S(1)} all-to-all(f32[16,1,4,512]{3,2,1,0:T(4,128)S(1)} %constant_dynamic-update-slice_fusion), channel_id=1, replica_groups=mesh['row'=8,'col'=16] {'col'}, dimensions={0} | all-to-all | bytes 262144 | tf_op jit(solution)/shard_map/all_to_all | solution.py:13
  279.0 56.7 %reduce-scatter.9.cloned.1.call-done = f32[1,64,512]{2,1,0:T(8,128)} async-done(((f32[1,512,512]{2,1,0:T(8,128)}), f32[1,64,512]{2,1,0:T(8,128)}) %reduce-scatter.9.cloned.1.call-update) | async-done | bytes 131088 | tf_op jit(solution)/shard_map/reduce_scatter | solution.py:95
  336.7 66.3 %all-reduce = (f32[512]{0:T(512)S(1)}, f32[512]{0:T(512)S(1)}) all-reduce(f32[512]{0:T(512)S(1)} %get-tuple-element.4, f32[512]{0:T(512)S(1)} %get-tuple-element.3), channel_id=1, replica_groups=mesh['row'=8,'col'=16] {'row','col'}, use_global_device_ids=true, to_apply=%region_1.0 | all-reduce | flops 1024 | bytes 8192 | tf_op jit(solution)/shard_map/psum | solution.py:107
  404.0 62.5 %psum.88 = f32[512]{0:T(512)S(1)} all-reduce(f32[512]{0:T(512)S(1)} %get-tuple-element.15), channel_id=1, replica_groups=mesh['row'=8,'col'=16] {'row','col'}, use_global_device_ids=true, to_apply=%region_9.11 | all-reduce | flops 512 | bytes 4096 | tf_op jit(solution)/shard_map/psum | solution.py:107
  467.3 43.6 %all-gather.6.cloned.1.call-done = f32[1,512,512]{2,1,0:T(8,128)} async-done(((f32[1,64,512]{2,1,0:T(8,128)}), f32[1,512,512]{2,1,0:T(8,128)}) %all-gather.6.cloned.1.call-update) | async-done | bytes 1048592 | tf_op jit(solution)/shard_map/all_gather | solution.py:87
  510.9 3.0 broadcast_select_fusion.3
  514.1 2.2 gather_fusion.5
  516.3 2.3 gather_fusion.4
  518.6 3.6 fusion.36
  522.2 2.2 fusion.12
  525.8 2.5 stack.195
  530.4 2.2 fusion.14
  536.1 2.6 copy.150
  538.7 98.3 %all-reduce.10.cloned.1.call-done = (f32[4,128,512]{2,1,0:T(8,128)}, f32[4,128,512]{2,1,0:T(8,128)}) async-done(((f32[4,128,512]{2,1,0:T(8,128)}, f32[4,128,512]{2,1,0:T(8,128)}), (f32[4,128,512]{2,1,0:T(8,128)}, f32[4,128,512]{2,1,0:T(8,128)})) %all-reduce.10.cloned.1.call-update) | async-done | bytes 2097168 | tf_op jit(solution)/shard_map/psum | solution.py:28
  637.0 2.4 gather_fusion.7
  639.4 3.3 gather_fusion.6
  642.8 2.1 fusion.32
  645.0 3.2 fusion.8
  648.2 2.2 fusion.34
  650.3 50.0 %reduce-scatter.11.cloned.1.call-done = f32[2,8,1,4,512]{4,1,3,0,2:T(8,128)} async-done(((f32[2,8,16,4,512]{4,1,3,0,2:T(8,128)}), f32[2,8,1,4,512]{4,1,3,0,2:T(8,128)}) %reduce-scatter.11.cloned.1.call-update) | async-done | bytes 131088 | tf_op jit(solution)/shard_map/reduce_scatter | solution.py:97
  702.0 6.6 all-to-all-start.2
  708.6 3.5 fusion.51
  713.5 2.1 all-to-all-done.2
  726.9 14.4 %all_to_all.31 = f32[16,1,4,512]{3,2,1,0:T(4,128)S(1)} all-to-all(f32[16,1,4,512]{3,2,1,0:T(4,128)S(1)} %constant_dynamic-update-slice_fusion.16), channel_id=1, replica_groups=mesh['row'=8,'col'=16] {'col'}, dimensions={0} | all-to-all | bytes 262144 | tf_op jit(solution)/shard_map/all_to_all | solution.py:13
  741.4 45.2 %reduce-scatter.13.cloned.1.call-done = f32[1,64,512]{2,1,0:T(8,128)} async-done(((f32[1,512,512]{2,1,0:T(8,128)}), f32[1,64,512]{2,1,0:T(8,128)}) %reduce-scatter.13.cloned.1.call-update) | async-done | bytes 131088 | tf_op jit(solution)/shard_map/reduce_scatter | solution.py:95
  787.5 66.3 %psum.91 = f32[512]{0:T(512)S(1)} all-reduce(f32[512]{0:T(512)S(1)} %multiply_reduce_fusion.2), channel_id=1, replica_groups=mesh['row'=8,'col'=16] {'row','col'}, use_global_device_ids=true, to_apply=%region_15.17 | all-reduce | flops 512 | bytes 4096 | tf_op jit(solution)/shard_map/psum | solution.py:117
  854.8 62.6 %psum.92 = f32[512]{0:T(512)S(1)} all-reduce(f32[512]{0:T(512)S(1)} %get-tuple-element.13), channel_id=1, replica_groups=mesh['row'=8,'col'=16] {'row','col'}, use_global_device_ids=true, to_apply=%region_17.19 | all-reduce | flops 512 | bytes 4096 | tf_op jit(solution)/shard_map/psum | solution.py:107
  918.1 43.7 %all-gather.8.cloned.1.call-done = f32[1,512,512]{2,1,0:T(8,128)} async-done(((f32[1,64,512]{2,1,0:T(8,128)}), f32[1,512,512]{2,1,0:T(8,128)}) %all-gather.8.cloned.1.call-update) | async-done | bytes 1048592 | tf_op jit(solution)/shard_map/all_gather | solution.py:87
  961.9 3.0 broadcast_select_fusion.1
  965.1 2.2 gather_fusion.9
  967.3 2.3 gather_fusion.8
  969.6 3.6 fusion.28
  973.2 2.2 fusion.4
  976.8 2.5 stack.215
  981.4 2.2 fusion.6
  987.0 2.6 copy.161
  989.6 98.4 %all-reduce.8.cloned.1.call-done = (f32[4,128,512]{2,1,0:T(8,128)}, f32[4,128,512]{2,1,0:T(8,128)}) async-done(((f32[4,128,512]{2,1,0:T(8,128)}, f32[4,128,512]{2,1,0:T(8,128)}), (f32[4,128,512]{2,1,0:T(8,128)}, f32[4,128,512]{2,1,0:T(8,128)})) %all-reduce.8.cloned.1.call-update) | async-done | bytes 2097168 | tf_op jit(solution)/shard_map/psum | solution.py:28
  1088.0 2.2 gather_fusion.11
  1090.2 3.3 gather_fusion.10
  1093.5 2.1 fusion.24
  1095.7 3.2 fusion
  1099.0 2.1 fusion.26
  1101.1 50.1 %reduce-scatter.15.cloned.1.call-done = f32[2,8,1,4,512]{4,1,3,0,2:T(8,128)} async-done(((f32[2,8,16,4,512]{4,1,3,0,2:T(8,128)}), f32[2,8,1,4,512]{4,1,3,0,2:T(8,128)}) %reduce-scatter.15.cloned.1.call-update) | async-done | bytes 131088 | tf_op jit(solution)/shard_map/reduce_scatter | solution.py:97
  1152.9 6.6 all-to-all-start.4
  1159.5 3.5 fusion.54
  1166.5 14.2 %all_to_all.32 = f32[16,1,4,512]{3,2,1,0:T(4,128)S(1)} all-to-all(f32[16,1,4,512]{3,2,1,0:T(4,128)S(1)} %constant_dynamic-update-slice_fusion.32), channel_id=1, replica_groups=mesh['row'=8,'col'=16] {'col'}, dimensions={0} | all-to-all | bytes 262144 | tf_op jit(solution)/shard_map/all_to_all | solution.py:13
  1180.8 56.8 %reduce-scatter.17.cloned.1.call-done = f32[1,64,512]{2,1,0:T(8,128)} async-done(((f32[1,512,512]{2,1,0:T(8,128)}), f32[1,64,512]{2,1,0:T(8,128)}) %reduce-scatter.17.cloned.1.call-update) | async-done | bytes 131088 | tf_op jit(solution)/shard_map/reduce_scatter | solution.py:95
  1238.5 66.3 %psum.95 = f32[512]{0:T(512)S(1)} all-reduce(f32[512]{0:T(512)S(1)} %multiply_reduce_fusion), channel_id=1, replica_groups=mesh['row'=8,'col'=16] {'row','col'}, use_global_device_ids=true, to_apply=%region_23.25 | all-reduce | flops 512 | bytes 4096 | tf_op jit(solution)/shard_map/psum | solution.py:117
  (220 shorter events, 59.6 us)
Async XLA Ops:
  7.2 52.8 %all-gather.4.cloned.1.call-start = ((), (), s32[]{:S(2)}) async-start(), calls=%async_computation.12 | async-start | bytes 1179648 | tf_op jit(solution)/shard_map/all_gather | solution.py:87
  7.9 178.2 %all-reduce.12.cloned.1.call-start = ((), (), s32[]{:S(2)}) async-start(), calls=%async_computation.23 | async-start | bytes 4194304 | tf_op jit(solution)/shard_map/psum | solution.py:28
  9.9 53.8 %copy-start.36 = (s32[2,1,8,2]{2,3,1,0:T(2,128)S(1)}, s32[2,1,8,2]{2,3,1,0:T(2,128)}, u32[]{:S(2)}) copy-start(s32[2,1,8,2]{2,3,1,0:T(2,128)} %param.8) | copy-start | bytes 388
  60.0 3.9 copy-start.1
  63.0 186.4 %reduce-scatter.7.cloned.1.call-start = ((), (), s32[]{:S(2)}) async-start(), calls=%async_computation.13 | async-start | bytes 2228224 | tf_op jit(solution)/shard_map/reduce_scatter | solution.py:97
  63.7 2.2 copy-start.30
  63.7 11.7 copy-start.27
  63.7 127.8 %copy-start.24 = (pred[8]{0:T(512)(128)(4,1)}, pred[8]{0:T(512)(128)(4,1)S(1)}, u32[]{:S(2)}) copy-start(pred[8]{0:T(512)(128)(4,1)S(1)} %get-tuple-element.39) | copy-start | bytes 28
  63.7 133.2 %copy-start.21 = (pred[8]{0:T(512)(128)(4,1)}, pred[8]{0:T(512)(128)(4,1)S(1)}, u32[]{:S(2)}) copy-start(pred[8]{0:T(512)(128)(4,1)S(1)} %get-tuple-element.17) | copy-start | bytes 28
  63.8 2.1 copy-start.49
  63.8 9.6 copy-start.48
  63.8 5.7 copy-start.43
  63.8 15.2 %copy-start.40 = (s32[8]{0:T(128)}, s32[8]{0:T(128)S(1)}, u32[]{:S(2)}) copy-start(s32[8]{0:T(128)S(1)} %get-tuple-element.34) | copy-start | bytes 100
  63.8 129.9 %copy-start.37 = (s32[8]{0:T(128)}, s32[8]{0:T(128)S(1)}, u32[]{:S(2)}) copy-start(s32[8]{0:T(128)S(1)} %get-tuple-element.35) | copy-start | bytes 100
  63.8 193.7 %copy-start.33 = (s32[8]{0:T(128)}, s32[8]{0:T(128)S(1)}, u32[]{:S(2)}) copy-start(s32[8]{0:T(128)S(1)} %get-tuple-element.33) | copy-start | bytes 100
  63.9 2.1 copy-start
  81.3 1.7 copy-start.10
  87.3 101.0 %copy-start.47 = (s32[1024]{0:T(1024)}, s32[1024]{0:T(1024)S(1)}, u32[]{:S(2)}) copy-start(s32[1024]{0:T(1024)S(1)} %get-tuple-element.45) | copy-start | bytes 12292
  87.3 101.0 %copy-start.46 = (s32[1024]{0:T(1024)}, s32[1024]{0:T(1024)S(1)}, u32[]{:S(2)}) copy-start(s32[1024]{0:T(1024)S(1)} %get-tuple-element.46) | copy-start | bytes 12292
  193.7 3.3 copy-start.7
  251.0 13.4 %all-to-all-start = ((f32[16,4,512]{2,1,0:T(4,128)}), f32[16,4,512]{2,1,0:T(4,128)S(1)}, u32[]{:S(2)}, u32[]{:S(2)}) async-start(f32[16,4,512]{2,1,0:T(4,128)} %bitcast.13), calls=%async_computation.1 | async-start | bytes 262144 | tf_op jit(solution)/shard_map/all_to_all | solution.py:101
  257.5 78.2 %reduce-scatter.9.cloned.1.call-start = ((), (), s32[]{:S(2)}) async-start(), calls=%async_computation.14 | async-start | bytes 1179648 | tf_op jit(solution)/shard_map/reduce_scatter | solution.py:95
  261.0 74.7 %copy-start.13 = (f32[1,64,512]{2,1,0:T(8,128)S(1)}, f32[1,64,512]{2,1,0:T(8,128)}, u32[]{:S(2)}) copy-start(f32[1,64,512]{2,1,0:T(8,128)} %param.6) | copy-start | bytes 393220
  262.4 248.5 %all-gather.6.cloned.1.call-start = ((), (), s32[]{:S(2)}) async-start(), calls=%async_computation.15 | async-start | bytes 1179648 | tf_op jit(solution)/shard_map/all_gather | solution.py:87
  467.2 169.8 %all-reduce.10.cloned.1.call-start = ((), (), s32[]{:S(2)}) async-start(), calls=%async_computation.22 | async-start | bytes 4194304 | tf_op jit(solution)/shard_map/psum | solution.py:28
  510.9 3.2 copy-start.3
  513.9 186.5 %reduce-scatter.11.cloned.1.call-start = ((), (), s32[]{:S(2)}) async-start(), calls=%async_computation.16 | async-start | bytes 2228224 | tf_op jit(solution)/shard_map/reduce_scatter | solution.py:97
  516.3 2.3 copy-start.31
  518.6 3.6 copy-start.44
  524.4 3.9 copy-start.6
  524.4 3.9 copy-start.28
  528.4 2.0 copy-start.41
  532.6 1.7 copy-start.12
  639.4 3.3 copy-start.25
  642.8 2.2 copy-start.38
  644.9 3.3 copy-start.8
  644.9 3.2 copy-start.22
  648.2 60.4 %copy-start.34 = (s32[8]{0:T(128)S(1)}, s32[8]{0:T(128)}, u32[]{:S(2)}) copy-start(s32[8]{0:T(128)} %copy-done.33) | copy-start | bytes 100
  702.0 13.6 %all-to-all-start.2 = ((f32[16,4,512]{2,1,0:T(4,128)}), f32[16,4,512]{2,1,0:T(4,128)}, u32[]{:S(2)}, u32[]{:S(2)}) async-start(f32[16,4,512]{2,1,0:T(4,128)} %bitcast.38), calls=%async_computation.5 | async-start | bytes 262144 | tf_op jit(solution)/shard_map/all_to_all | solution.py:101
  708.6 78.0 %reduce-scatter.13.cloned.1.call-start = ((), (), s32[]{:S(2)}) async-start(), calls=%async_computation.17 | async-start | bytes 1179648 | tf_op jit(solution)/shard_map/reduce_scatter | solution.py:95
  712.1 74.5 %copy-start.9 = (f32[1,64,512]{2,1,0:T(8,128)S(1)}, f32[1,64,512]{2,1,0:T(8,128)}, u32[]{:S(2)}) copy-start(f32[1,64,512]{2,1,0:T(8,128)} %multiply_add_fusion.2) | copy-start | bytes 393220
  713.5 248.4 %all-gather.8.cloned.1.call-start = ((), (), s32[]{:S(2)}) async-start(), calls=%async_computation.18 | async-start | bytes 1179648 | tf_op jit(solution)/shard_map/all_gather | solution.py:87
  853.8 64.3 %copy-start.17 = (f32[512]{0:T(512)}, f32[512]{0:T(512)S(1)}, u32[]{:S(2)}) copy-start(f32[512]{0:T(512)S(1)} %div.17) | copy-start | bytes 6148
  854.8 63.3 %copy-start.15 = (f32[1,64,512]{2,1,0:T(8,128)}, f32[1,64,512]{2,1,0:T(8,128)S(1)}, u32[]{:S(2)}) copy-start(f32[1,64,512]{2,1,0:T(8,128)S(1)} %get-tuple-element.14) | copy-start | bytes 393220
  918.1 169.9 %all-reduce.8.cloned.1.call-start = ((), (), s32[]{:S(2)}) async-start(), calls=%async_computation.21 | async-start | bytes 4194304 | tf_op jit(solution)/shard_map/psum | solution.py:28
  961.9 3.2 copy-start.2
  964.9 186.4 %reduce-scatter.15.cloned.1.call-start = ((), (), s32[]{:S(2)}) async-start(), calls=%async_computation.19 | async-start | bytes 2228224 | tf_op jit(solution)/shard_map/reduce_scatter | solution.py:97
  967.3 2.3 copy-start.32
  969.6 3.6 copy-start.45
  975.4 3.9 copy-start.4
  975.4 3.9 copy-start.29
  979.3 2.0 copy-start.42
  983.6 1.7 copy-start.11
  1090.2 3.3 copy-start.26
  1093.5 2.2 copy-start.39
  1095.7 3.2 copy-start.5
  1095.7 3.2 copy-start.23
  1099.0 60.5 %copy-start.35 = (s32[8]{0:T(128)S(1)}, s32[8]{0:T(128)}, u32[]{:S(2)}) copy-start(s32[8]{0:T(128)} %copy-done.33) | copy-start | bytes 100
  1152.9 13.5 %all-to-all-start.4 = ((f32[16,4,512]{2,1,0:T(4,128)}), f32[16,4,512]{2,1,0:T(4,128)S(1)}, u32[]{:S(2)}, u32[]{:S(2)}) async-start(f32[16,4,512]{2,1,0:T(4,128)} %bitcast.61), calls=%async_computation.9 | async-start | bytes 262144 | tf_op jit(solution)/shard_map/all_to_all | solution.py:101
  1159.4 78.1 %reduce-scatter.17.cloned.1.call-start = ((), (), s32[]{:S(2)}) async-start(), calls=%async_computation.20 | async-start | bytes 1179648 | tf_op jit(solution)/shard_map/reduce_scatter | solution.py:95
  1163.0 74.6 %copy-start.14 = (f32[1,64,512]{2,1,0:T(8,128)S(1)}, f32[1,64,512]{2,1,0:T(8,128)}, u32[]{:S(2)}) copy-start(f32[1,64,512]{2,1,0:T(8,128)} %multiply_add_fusion.1) | copy-start | bytes 393220
  1163.0 141.9 %copy-start.20 = (f32[512]{0:T(512)S(1)}, f32[512]{0:T(512)}, u32[]{:S(2)}) copy-start(f32[512]{0:T(512)} %copy-done.19) | copy-start | bytes 6148
  1163.0 141.9 %copy-start.16 = (f32[1,64,512]{2,1,0:T(8,128)S(1)}, f32[1,64,512]{2,1,0:T(8,128)}, u32[]{:S(2)}) copy-start(f32[1,64,512]{2,1,0:T(8,128)} %copy-done.15) | copy-start | bytes 393220
  1163.0 141.9 %copy-start.18 = (f32[512]{0:T(512)S(1)}, f32[512]{0:T(512)}, u32[]{:S(2)}) copy-start(f32[512]{0:T(512)} %copy-done.17) | copy-start | bytes 6148
  (1 other events, 0.8 us)
Sparse Core Ops, SparseCore 0:
  10.3 49.5 all-gather.3
  63.1 122.9 all-reduce.11
  188.5 60.8 reduce-scatter.6
  262.5 73.1 reduce-scatter.8
  467.3 43.4 all-gather.5
  514.0 122.9 all-reduce.9
  639.5 60.8 reduce-scatter.10
  713.6 72.9 reduce-scatter.12
  918.2 43.6 all-gather.7
  965.0 122.9 all-reduce.7
  1090.4 60.8 reduce-scatter.14
  1164.5 73.0 reduce-scatter.16
